TPU v7x, 512 devices: a whole 4x8x8 slice. The times are simulated.
512 devices in a mesh: dp: 8 (over y), pipe: 4 (over z_lo), tensor: 16 (over z_hi, x, core).
Axes of the slice: x: 4, y: 8, z: 8 (z_hi: 2, z_lo: 4; z = z_hi * 4 + z_lo), core: 2. Of those that a mesh axis runs over, the one named last changes fastest.
Arguments:
- activations: bfloat16 [4, 1536, 4096], P('pipe', 'tensor', 'dp'), may hold values from -6 to 6
- upstream: bfloat16 [4, 1536, 4096], P('pipe', 'tensor', 'dp'), may hold values from -4 to 4
- gate_value: bfloat16 [4, 1536, 14336], P('pipe', 'dp', 'tensor'), may hold values from -6 to 6
- up_value: bfloat16 [4, 1536, 14336], P('pipe', 'dp', 'tensor'), may hold values from -6 to 6
- hidden_grad: bfloat16 [4, 1536, 14336], P('pipe', 'dp', 'tensor'), may hold values from -4 to 4
- gate_weight: bfloat16 [4, 4096, 14336], P('pipe', 'dp', 'tensor'), may hold values from -0.09375 to 0.09375
- up_weight: bfloat16 [4, 4096, 14336], P('pipe', 'dp', 'tensor'), may hold values from -0.09375 to 0.09375
- gate_mask: int32 [4, 32, 112], P('pipe', 'dp', 'tensor'), may hold values 0 or 1
- up_mask: int32 [4, 32, 112], P('pipe', 'dp', 'tensor'), may hold values 0 or 1
Outputs:
- gate_gradient: bfloat16 [4, 4096, 14336], P('pipe', 'dp', 'tensor')
- up_gradient: bfloat16 [4, 4096, 14336], P('pipe', 'dp', 'tensor')
- handed_back: bfloat16 [4, 1536, 4096], P('pipe', 'tensor', 'dp')
Inputs may be any that keep to these rules, and one draw needn't show every extreme that they name: gate_mask[s, i, j] keeps (1) or prunes (0) block (i, j) of gate_weight[s]. up_mask[s, i, j] keeps (1) or prunes (0) block (i, j) of up_weight[s].
All inputs are finite; a program needn't handle non-finite values.
Results may differ from a plain program's by a relative error of at most 0.0049.
Values may be sent and summed in bfloat16 or wider, within the bound.
A program may use at most 64 MiB of HBM per device.

v0:
```python
import jax
import jax.numpy as jnp
from jax import lax
from jax.sharding import PartitionSpec as P


def shifted(array, axis, by):
    devices = lax.axis_size(axis)
    pairs = [(i, i + by) for i in range(devices) if 0 <= i + by < devices]
    return lax.ppermute(array, axis, pairs)


def apply_blocks(matrix, keep_mask):
    rows_blocks, cols_blocks = keep_mask.shape
    shaped = matrix.reshape(
        rows_blocks, matrix.shape[0] // rows_blocks, cols_blocks, matrix.shape[1] // cols_blocks
    )
    return (shaped * keep_mask.astype(matrix.dtype)[:, None, :, None]).reshape(matrix.shape)


def per_device(
    activations,
    upstream,
    gate_value,
    up_value,
    hidden_grad,
    gate_weight,
    up_weight,
    gate_mask,
    up_mask,
):
    gathered = lax.all_gather(activations, "tensor", axis=1, tiled=True)[0]
    gate_float = gate_value[0].astype(jnp.float32)
    up_float = up_value[0].astype(jnp.float32)
    hidden_float = hidden_grad[0].astype(jnp.float32)
    gate_sigmoid = jax.nn.sigmoid(gate_float)
    up_delta = (hidden_float * gate_float * gate_sigmoid).astype(jnp.bfloat16)
    gate_delta = (
        hidden_float * up_float * gate_sigmoid * (1.0 + gate_float * (1.0 - gate_sigmoid))
    ).astype(jnp.bfloat16)
    gate_kept = apply_blocks(gate_weight[0], gate_mask[0])
    up_kept = apply_blocks(up_weight[0], up_mask[0])
    over_tokens = (((0,), (0,)), ((), ()))
    over_hidden = (((1,), (1,)), ((), ()))
    gate_piece = lax.all_gather(gate_delta, "dp", axis=0, tiled=True)
    up_piece = lax.all_gather(up_delta, "dp", axis=0, tiled=True)
    gate_acc = lax.dot_general(
        gathered, gate_piece, over_tokens, preferred_element_type=jnp.float32
    )
    up_acc = lax.dot_general(gathered, up_piece, over_tokens, preferred_element_type=jnp.float32)
    partial_rows = lax.dot_general(
        gate_piece, gate_kept, over_hidden, preferred_element_type=jnp.float32
    )
    partial_rows = partial_rows + lax.dot_general(
        up_piece, up_kept, over_hidden, preferred_element_type=jnp.float32
    )
    branch = partial_rows
    gate_acc, up_acc, branch = (gate_acc, up_acc, branch)
    own_rows = lax.psum_scatter(branch, "tensor", scatter_dimension=0, tiled=True)
    gate_gradient = apply_blocks(gate_acc, gate_mask[0]).astype(jnp.bfloat16)[None]
    up_gradient = apply_blocks(up_acc, up_mask[0]).astype(jnp.bfloat16)[None]
    section_grad = (upstream[0].astype(jnp.float32) + own_rows).astype(jnp.bfloat16)
    handed = shifted(section_grad, "pipe", -1)
    return (gate_gradient, up_gradient, handed[None])


def solution(mesh):
    return jax.shard_map(
        per_device,
        mesh=mesh,
        in_specs=(
            P("pipe", "tensor", "dp"),
            P("pipe", "tensor", "dp"),
            P("pipe", "dp", "tensor"),
            P("pipe", "dp", "tensor"),
            P("pipe", "dp", "tensor"),
            P("pipe", "dp", "tensor"),
            P("pipe", "dp", "tensor"),
            P("pipe", "dp", "tensor"),
            P("pipe", "dp", "tensor"),
        ),
        out_specs=(P("pipe", "dp", "tensor"), P("pipe", "dp", "tensor"), P("pipe", "tensor", "dp")),
        check_vma=False,
    )
```

profile of v0, /device:TPU:64, one launch (start us, length us, event | category | flops | bytes accessed | tf_op | source)
XLA Modules:
  0.0 296.9 jit_solution(10414191053938637605)
XLA Ops:
  7.2 0.0 all-gather.4.cloned.1.call-start
  7.2 2.5 fusion.29
  9.8 0.0 all-gather.4.cloned.1.call-update
  9.8 0.0 all-gather.8.cloned.1.call-start
  9.8 0.7 all-gather.8.cloned.1.call-update
  10.5 0.0 all-gather.6.cloned.1.call-start
  10.6 0.7 all-gather.6.cloned.1.call-update
  11.3 0.0 reduce-scatter.2.cloned.1.call-start
  11.3 0.8 convert_bitcast_fusion.3
  12.1 0.1 copy.19
  12.2 0.5 copy.18
  12.7 0.1 copy.21
  12.9 0.5 copy.20
  13.4 46.9 %all-gather.4.cloned.1.call-done = bf16[1536,896]{1,0:T(8,128)(2,1)} async-done(((bf16[192,896]{1,0:T(8,128)(2,1)}), bf16[1536,896]{1,0:T(8,128)(2,1)}) %all-gather.4.cloned.1.call-update) | async-done | bytes 2752528 | tf_op jit(solution)/shard_map/all_gather | solution.py:45
  60.3 0.3 mul.74
  60.6 5.3 %fusion.17 = f32[1536,512]{1,0:T(8,128)} fusion(bf16[1536,896]{1,0:T(8,128)(2,1)} %all-gather.4.cloned.1.call-done, bf16[112,8,4,128]{3,2,1,0:T(4,128)(2,1)S(1)} %bitcast.99, bf16[1,512,896]{1,2,0:T(8,128)(2,1)S(1)} %copy.18), kind=kOutput, calls=%fused_computation.17 | convolution fusion | flops 1409744896 | bytes 7733248 | tf_op jit(solution)/shard_map/dot_general | solution.py:51
  65.8 41.5 %all-gather.8.cloned.1.call-done = bf16[1536,896]{1,0:T(8,128)(2,1)} async-done(((bf16[192,896]{1,0:T(8,128)(2,1)}), bf16[1536,896]{1,0:T(8,128)(2,1)}) %all-gather.8.cloned.1.call-update) | async-done | bytes 2752528 | tf_op jit(solution)/shard_map/all_gather | solution.py:46
  107.3 0.3 mul.77
  107.6 6.2 %convolution_add_fusion = f32[1536,512]{1,0:T(8,128)} fusion(f32[1536,512]{1,0:T(8,128)} %fusion.17, bf16[1536,896]{1,0:T(8,128)(2,1)} %all-gather.8.cloned.1.call-done, bf16[112,8,4,128]{3,2,1,0:T(4,128)(2,1)S(1)} %bitcast.98, bf16[1,512,896]{1,2,0:T(8,128)(2,1)S(1)} %copy.20), kind=kOutput, calls=%fused_computation | convolution fusion | flops 1410531328 | bytes 10878976 | tf_op jit(solution)/shard_map/dot_general | solution.py:54
  113.9 0.1 copy.16
  114.0 0.1 copy.17
  114.1 58.1 %all-gather.6.cloned.1.call-done = bf16[1,1536,512]{2,1,0:T(8,128)(2,1)} async-done(((bf16[1,96,512]{2,1,0:T(8,128)(2,1)}), bf16[1,1536,512]{2,1,0:T(8,128)(2,1)}) %all-gather.6.cloned.1.call-update) | async-done | bytes 1572880 | tf_op jit(solution)/shard_map/all_gather | solution.py:32
  172.2 0.3 mul.66
  172.5 3.9 %fusion.10 = bf16[1,512,896]{1,2,0:T(8,128)(2,1)S(1)} fusion(f32[112,8,4,128]{3,2,1,0:T(4,128)S(1)} %bitcast.97, bf16[1536,896]{1,0:T(8,128)(2,1)} %all-gather.4.cloned.1.call-done, bf16[1,1536,512]{2,1,0:T(8,128)(2,1)} %all-gather.6.cloned.1.call-done), kind=kOutput, calls=%fused_computation.9 | convolution fusion | flops 1410203648 | bytes 7077888 | tf_op jit(solution)/shard_map/dot_general | solution.py:47
  176.4 100.5 %reduce-scatter.2.cloned.1.call-done = f32[96,512]{1,0:T(8,128)} async-done(((f32[1536,512]{1,0:T(8,128)}), f32[96,512]{1,0:T(8,128)}) %reduce-scatter.2.cloned.1.call-update) | async-done | bytes 196624 | tf_op jit(solution)/shard_map/reduce_scatter | solution.py:59
  276.9 0.9 fusion.30
  277.9 5.2 %collective-permute-start = (bf16[96,512]{1,0:T(8,128)(2,1)S(1)}, bf16[96,512]{1,0:T(8,128)(2,1)S(1)}, u32[]{:S(2)}, u32[]{:S(2)}) collective-permute-start(bf16[96,512]{1,0:T(8,128)(2,1)S(1)} %fusion.30), channel_id=1, source_target_pairs={{16,0},{32,16},{48,32},{17,1},{33,17},{49,33},{18,2},{34,18},{50,3... | collective-permute-start | bytes 294920 | tf_op jit(solution)/shard_map/ppermute | solution.py:10
  283.1 0.3 mul.71
  283.4 3.8 %fusion.13 = bf16[1,512,896]{1,2,0:T(8,128)(2,1)S(1)} fusion(f32[112,8,4,128]{3,2,1,0:T(4,128)S(1)} %bitcast.96, bf16[1536,896]{1,0:T(8,128)(2,1)} %all-gather.8.cloned.1.call-done, bf16[1,1536,512]{2,1,0:T(8,128)(2,1)} %all-gather.6.cloned.1.call-done), kind=kOutput, calls=%fused_computation.10 | convolution fusion | flops 1410203648 | bytes 7077888 | tf_op jit(solution)/shard_map/dot_general | solution.py:50
  287.2 1.3 copy.22
  288.5 1.3 copy.23
  289.8 0.6 copy.43
  (11 shorter events, 0.0 us)
Async XLA Ops:
  7.2 5.0 %copy-start = (bf16[1,512,896]{2,1,0:T(8,128)(2,1)S(1)}, bf16[1,512,896]{2,1,0:T(8,128)(2,1)}, u32[]{:S(2)}) copy-start(bf16[1,512,896]{2,1,0:T(8,128)(2,1)} %param.14) | copy-start | bytes 2752516
  7.2 5.5 %copy-start.3 = (s32[1,4,7]{2,1,0:T(4,128)S(1)}, s32[1,4,7]{2,1,0:T(4,128)}, u32[]{:S(2)}) copy-start(s32[1,4,7]{2,1,0:T(4,128)} %param.17) | copy-start | bytes 340
  7.2 5.7 %copy-start.1 = (bf16[1,512,896]{2,1,0:T(8,128)(2,1)S(1)}, bf16[1,512,896]{2,1,0:T(8,128)(2,1)}, u32[]{:S(2)}) copy-start(bf16[1,512,896]{2,1,0:T(8,128)(2,1)} %param.15) | copy-start | bytes 2752516
  7.2 53.1 %all-gather.4.cloned.1.call-start = ((), (), s32[]{:S(2)}) async-start(), calls=%async_computation.1 | async-start | bytes 3096576 | tf_op jit(solution)/shard_map/all_gather | solution.py:45
  9.8 97.5 %all-gather.8.cloned.1.call-start = ((), (), s32[]{:S(2)}) async-start(), calls=%async_computation.3 | async-start | bytes 3096576 | tf_op jit(solution)/shard_map/all_gather | solution.py:46
  10.5 161.7 %all-gather.6.cloned.1.call-start = ((), (), s32[]{:S(2)}) async-start(), calls=%async_computation.2 | async-start | bytes 1671168 | tf_op jit(solution)/shard_map/all_gather | solution.py:32
  11.3 265.7 %reduce-scatter.2.cloned.1.call-start = ((), (), s32[]{:S(2)}) async-start(), calls=%async_computation.4 | async-start | bytes 3342336 | tf_op jit(solution)/shard_map/reduce_scatter | solution.py:59
  172.5 104.4 %copy-start.2 = (bf16[1,96,512]{2,1,0:T(8,128)(2,1)S(1)}, bf16[1,96,512]{2,1,0:T(8,128)(2,1)}, u32[]{:S(2)}) copy-start(bf16[1,96,512]{2,1,0:T(8,128)(2,1)} %param.10) | copy-start | bytes 294916
  277.9 11.9 %collective-permute-start = (bf16[96,512]{1,0:T(8,128)(2,1)S(1)}, bf16[96,512]{1,0:T(8,128)(2,1)S(1)}, u32[]{:S(2)}, u32[]{:S(2)}) collective-permute-start(bf16[96,512]{1,0:T(8,128)(2,1)S(1)} %fusion.30), channel_id=1, source_target_pairs={{16,0},{32,16},{48,32},{17,1},{33,17},{49,33},{18,2},{34,18},{50,3... | collective-permute-start | bytes 294920 | tf_op jit(solution)/shard_map/ppermute | solution.py:10
Sparse Core Ops, SparseCore 0:
  10.7 49.5 all-gather.3
  62.9 44.3 all-gather.7
  110.6 61.5 all-gather.5
  176.9 99.9 reduce-scatter.1
where the time goes:
time: 297 us
  waiting for transfers between devices  248 us (84%)
  matrix products  19.2 us (6%)
  between operations  13.9 us (5%)
  local copies, waits for them, and re-layouts  5.86 us (2%)
  starting transfers between devices  5.31 us (2%)
  other arithmetic  4.23 us (1%)
    reduce_scatter x1, waiting for transfers between devices, per_device(): lax.psum_scatter(branch, 'tensor', scatter_dimension=0, tiled=True)  101 us
    all_gather x1, waiting for transfers between devices, per_device(): gathered = lax.all_gather(activations, 'tensor', axis=1, tiled=True)[0]  58.1 us
    all_gather x1, waiting for transfers between devices, per_device(): gate_piece = lax.all_gather(gate_delta, 'dp', axis=0, tiled=True)  46.9 us
    all_gather x1, waiting for transfers between devices, per_device(): up_piece = lax.all_gather(up_delta, 'dp', axis=0, tiled=True)  41.5 us
    dot_general x1, matrix products, per_device(): lax.dot_general(up_piece, up_kept, over_hidden, preferred_element_type=jn...  6.21 us
  transfers between devices with their start and end apart: 5, of which 4 were waited for; matrix products, arithmetic and copies ran while one was open for 8% of the time, Pallas kernels for 0%

commit v1 on v0

--- a/solution.py
+++ b/solution.py
@@ -42,7 +42,9 @@
     up_kept = apply_blocks(up_weight[0], up_mask[0])
     over_tokens = (((0,), (0,)), ((), ()))
     over_hidden = (((1,), (1,)), ((), ()))
-    gate_piece = lax.all_gather(gate_delta, "dp", axis=0, tiled=True)
+    gate_piece = jnp.concatenate(
+        lax.all_to_all(jnp.stack([gate_delta] * lax.axis_size("dp")), "dp", 0, 0), axis=0
+    )
     up_piece = lax.all_gather(up_delta, "dp", axis=0, tiled=True)
     gate_acc = lax.dot_general(
         gathered, gate_piece, over_tokens, preferred_element_type=jnp.float32

time: 297 us -> 301 us (1.013)
  starting transfers between devices: 5.31 us -> 12.5 us
  waiting for transfers between devices: 248 us -> 242 us
  local copies, waits for them, and re-layouts: 5.86 us -> 9.79 us
    all_to_all x0 -> x1, waiting for transfers between devices: none -> 85.8 us  [per_device(): lax.all_to_all(jnp.stack([gate_delta] * lax.axis_size('dp')), 'dp', 0, 0)]
    all_gather x1 -> x0, waiting for transfers between devices: 46.9 us -> none  [per_device(): gate_piece = lax.all_gather(gate_delta, 'dp', axis=0, tiled=True)]
    all_gather x1, waiting for transfers between devices: 41.5 us -> 0.01 us  [per_device(): up_piece = lax.all_gather(up_delta, 'dp', axis=0, tiled=True)]
    all_to_all x0 -> x1, starting transfers between devices: none -> 7.23 us  [per_device(): lax.all_to_all(jnp.stack([gate_delta] * lax.axis_size('dp')), 'dp', 0, 0)]
    all_gather x1, waiting for transfers between devices: 58.1 us -> 54.7 us  [per_device(): gathered = lax.all_gather(activations, 'tensor', axis=1, tiled=True)[0]]
  transfers between devices with their start and end apart: 5 -> 5, of which waited for: 4 -> 3; matrix products, arithmetic and copies ran while one was open for 8% -> 9% of each run, Pallas kernels for 0% -> 0%
where the time goes in v1:
time: 301 us
  waiting for transfers between devices  242 us (80%)
  matrix products  19.4 us (6%)
  between operations  13.9 us (5%)
  starting transfers between devices  12.5 us (4%)
  local copies, waits for them, and re-layouts  9.79 us (3%)
  other arithmetic  3.27 us (1%)
    reduce_scatter x1, waiting for transfers between devices, per_device(): lax.psum_scatter(branch, 'tensor', scatter_dimension=0, tiled=True)  101 us
    all_to_all x1, waiting for transfers between devices, per_device(): lax.all_to_all(jnp.stack([gate_delta] * lax.axis_size('dp')), 'dp', 0, 0)  85.8 us
    all_gather x1, waiting for transfers between devices, per_device(): gathered = lax.all_gather(activations, 'tensor', axis=1, tiled=True)[0]  54.7 us
    all_to_all x1, starting transfers between devices, per_device(): lax.all_to_all(jnp.stack([gate_delta] * lax.axis_size('dp')), 'dp', 0, 0)  7.23 us
    dot_general x1, matrix products, per_device(): lax.dot_general(up_piece, up_kept, over_hidden, preferred_element_type=jn...  6.2 us
  transfers between devices with their start and end apart: 5, of which 3 were waited for; matrix products, arithmetic and copies ran while one was open for 9% of the time, Pallas kernels for 0%

profile of v1, /device:TPU:64, one launch (start us, length us, event | category | flops | bytes accessed | tf_op | source)
XLA Modules:
  0.0 300.8 jit_solution(2910156814967458798)
XLA Ops:
  7.2 0.0 all-gather.6.cloned.1.call-start
  7.2 2.3 fusion.35
  9.5 0.0 all-gather.6.cloned.1.call-update
  9.5 1.9 stack.5
  11.4 7.2 %all-to-all-start = ((bf16[8,192,896]{2,1,0:T(8,128)(2,1)}), bf16[8,192,896]{2,1,0:T(8,128)(2,1)}, u32[]{:S(2)}, u32[]{:S(2)}) async-start(bf16[8,192,896]{2,1,0:T(8,128)(2,1)} %stack.5), calls=%async_computation | async-start | bytes 5505024 | tf_op jit(solution)/shard_map/all_to_all | solution.py:46
  18.7 0.0 all-gather.4.cloned.1.call-start
  18.8 0.7 all-gather.4.cloned.1.call-update
  19.5 0.0 reduce-scatter.2.cloned.1.call-start
  19.5 0.1 copy.18
  19.6 0.3 mul.85
  19.9 1.3 mul.86
  21.2 1.3 copy.19
  22.5 0.1 copy.21
  22.6 0.5 copy.20
  23.2 85.8 %all-to-all-done = bf16[8,192,896]{2,1,0:T(8,128)(2,1)} async-done(((bf16[8,192,896]{2,1,0:T(8,128)(2,1)}), bf16[8,192,896]{2,1,0:T(8,128)(2,1)}, u32[]{:S(2)}, u32[]{:S(2)}) %all-to-all-start) | async-done | bytes 2752544 | tf_op jit(solution)/shard_map/all_to_all | solution.py:46
  109.0 5.5 %fusion.24 = f32[1536,512]{1,0:T(8,128)} fusion(bf16[1536,896]{1,0:T(8,128)(2,1)} %bitcast.1, bf16[1,512,896]{1,2,0:T(8,128)(2,1)} %copy.19, bf16[1,512,896]{1,2,0:T(8,128)(2,1)S(1)} %copy-done.2), kind=kOutput, calls=%fused_computation.19 | convolution fusion | flops 1409744896 | bytes 7733248 | tf_op jit(solution)/shard_map/dot_general | solution.py:53
  114.5 0.3 mul.89
  114.8 6.2 %convolution_add_fusion = f32[1536,512]{1,0:T(8,128)} fusion(f32[1536,512]{1,0:T(8,128)} %fusion.24, bf16[1,1536,896]{2,1,0:T(8,128)(2,1)} %all-gather.6.cloned.1.call-done, bf16[112,8,4,128]{3,2,1,0:T(4,128)(2,1)S(1)} %bitcast.90, bf16[1,512,896]{1,2,0:T(8,128)(2,1)S(1)} %copy.20), kind=kOutput, calls=%fused_computation | convolution fusion | flops 1410531328 | bytes 10878976 | tf_op jit(solution)/shard_map/dot_general | solution.py:56
  121.0 0.0 reduce-scatter.2.cloned.1.call-update
  121.0 0.1 copy.16
  121.1 0.1 copy.17
  121.2 54.7 %all-gather.4.cloned.1.call-done = bf16[1,1536,512]{2,1,0:T(8,128)(2,1)} async-done(((bf16[1,96,512]{2,1,0:T(8,128)(2,1)}), bf16[1,1536,512]{2,1,0:T(8,128)(2,1)}) %all-gather.4.cloned.1.call-update) | async-done | bytes 1572880 | tf_op jit(solution)/shard_map/all_gather | solution.py:32
  175.9 0.3 mul.76
  176.2 3.9 %fusion.14 = bf16[1,512,896]{1,2,0:T(8,128)(2,1)S(1)} fusion(f32[112,8,4,128]{3,2,1,0:T(4,128)S(1)} %bitcast.89, bf16[1536,896]{1,0:T(8,128)(2,1)} %bitcast.1, bf16[1,1536,512]{2,1,0:T(8,128)(2,1)} %all-gather.4.cloned.1.call-done), kind=kOutput, calls=%fused_computation.11 | convolution fusion | flops 1410203648 | bytes 7077888 | tf_op jit(solution)/shard_map/dot_general | solution.py:49
  180.1 100.7 %reduce-scatter.2.cloned.1.call-done = f32[96,512]{1,0:T(8,128)} async-done(((f32[1536,512]{1,0:T(8,128)}), f32[96,512]{1,0:T(8,128)}) %reduce-scatter.2.cloned.1.call-update) | async-done | bytes 196624 | tf_op jit(solution)/shard_map/reduce_scatter | solution.py:61
  280.8 0.9 fusion.37
  281.7 5.2 %collective-permute-start = (bf16[96,512]{1,0:T(8,128)(2,1)S(1)}, bf16[96,512]{1,0:T(8,128)(2,1)S(1)}, u32[]{:S(2)}, u32[]{:S(2)}) collective-permute-start(bf16[96,512]{1,0:T(8,128)(2,1)S(1)} %fusion.37), channel_id=1, source_target_pairs={{16,0},{32,16},{48,32},{17,1},{33,17},{49,33},{18,2},{34,18},{50,3... | collective-permute-start | bytes 294920 | tf_op jit(solution)/shard_map/ppermute | solution.py:10
  286.9 0.3 mul.82
  287.2 3.9 %fusion.17 = bf16[1,512,896]{1,2,0:T(8,128)(2,1)S(1)} fusion(f32[112,8,4,128]{3,2,1,0:T(4,128)S(1)} %bitcast.88, bf16[1,1536,512]{2,1,0:T(8,128)(2,1)} %all-gather.4.cloned.1.call-done, bf16[1,1536,896]{2,1,0:T(8,128)(2,1)} %all-gather.6.cloned.1.call-done), kind=kOutput, calls=%fused_computation.12 | convolution fusion | flops 1410203648 | bytes 7077888 | tf_op jit(solution)/shard_map/dot_general | solution.py:52
  291.1 1.3 copy.22
  292.4 1.3 copy.23
  293.6 0.6 copy.38
  (16 shorter events, 0.0 us)
Async XLA Ops:
  7.2 107.3 %all-gather.6.cloned.1.call-start = ((), (), s32[]{:S(2)}) async-start(), calls=%async_computation.4 | async-start | bytes 3096576 | tf_op jit(solution)/shard_map/all_gather | solution.py:48
  11.4 8.1 %copy-start.4 = (s32[1,4,7]{2,1,0:T(4,128)S(1)}, s32[1,4,7]{2,1,0:T(4,128)}, u32[]{:S(2)}) copy-start(s32[1,4,7]{2,1,0:T(4,128)} %param.16) | copy-start | bytes 340
  11.4 97.5 %all-to-all-start = ((bf16[8,192,896]{2,1,0:T(8,128)(2,1)}), bf16[8,192,896]{2,1,0:T(8,128)(2,1)}, u32[]{:S(2)}, u32[]{:S(2)}) async-start(bf16[8,192,896]{2,1,0:T(8,128)(2,1)} %stack.5), calls=%async_computation | async-start | bytes 5505024 | tf_op jit(solution)/shard_map/all_to_all | solution.py:46
  18.7 2.5 copy-start
  18.7 3.8 %copy-start.5 = (s32[1,4,7]{2,1,0:T(4,128)S(1)}, s32[1,4,7]{2,1,0:T(4,128)}, u32[]{:S(2)}) copy-start(s32[1,4,7]{2,1,0:T(4,128)} %param.17) | copy-start | bytes 340
  18.7 3.9 %copy-start.1 = (bf16[1,512,896]{2,1,0:T(8,128)(2,1)S(1)}, bf16[1,512,896]{2,1,0:T(8,128)(2,1)}, u32[]{:S(2)}) copy-start(bf16[1,512,896]{2,1,0:T(8,128)(2,1)} %param.15) | copy-start | bytes 2752516
  18.7 157.2 %all-gather.4.cloned.1.call-start = ((), (), s32[]{:S(2)}) async-start(), calls=%async_computation.2 | async-start | bytes 1671168 | tf_op jit(solution)/shard_map/all_gather | solution.py:32
  19.5 261.3 %reduce-scatter.2.cloned.1.call-start = ((), (), s32[]{:S(2)}) async-start(), calls=%async_computation.3 | async-start | bytes 3342336 | tf_op jit(solution)/shard_map/reduce_scatter | solution.py:61
  21.2 87.8 %copy-start.2 = (bf16[1,512,896]{1,2,0:T(8,128)(2,1)S(1)}, bf16[1,512,896]{1,2,0:T(8,128)(2,1)}, u32[]{:S(2)}) copy-start(bf16[1,512,896]{1,2,0:T(8,128)(2,1)} %mul.86) | copy-start | bytes 2752516
  176.2 104.6 %copy-start.3 = (bf16[1,96,512]{2,1,0:T(8,128)(2,1)S(1)}, bf16[1,96,512]{2,1,0:T(8,128)(2,1)}, u32[]{:S(2)}) copy-start(bf16[1,96,512]{2,1,0:T(8,128)(2,1)} %param.10) | copy-start | bytes 294916
  281.7 11.9 %collective-permute-start = (bf16[96,512]{1,0:T(8,128)(2,1)S(1)}, bf16[96,512]{1,0:T(8,128)(2,1)S(1)}, u32[]{:S(2)}, u32[]{:S(2)}) collective-permute-start(bf16[96,512]{1,0:T(8,128)(2,1)S(1)} %fusion.37), channel_id=1, source_target_pairs={{16,0},{32,16},{48,32},{17,1},{33,17},{49,33},{18,2},{34,18},{50,3... | collective-permute-start | bytes 294920 | tf_op jit(solution)/shard_map/ppermute | solution.py:10
Sparse Core Ops, SparseCore 0:
  10.1 96.2 all-gather.5
  109.7 66.1 all-gather.3
  180.8 99.9 reduce-scatter.1
